TPU v7x, 256 devices: a whole 4x4x8 slice. The times are simulated.
256 devices in a mesh: seq: 32 (over z, y_hi, core), tp: 8 (over y_lo, x).
Axes of the slice: x: 4, y: 4 (y_hi: 2, y_lo: 2; y = y_hi * 2 + y_lo), z: 8, core: 2. Of those that a mesh axis runs over, the one named last changes fastest.
Arguments:
- queries: bfloat16 [8192, 5120], P('seq', 'tp'), may hold values from -120 to 120, as said below
- prompt_keys: bfloat16 [4096, 1024], P('seq', 'tp'), may hold values from -4 to 4
- prompt_values: bfloat16 [4096, 1024], P('seq', 'tp'), may hold values from -6 to 6
- response_keys: bfloat16 [8192, 1024], P('seq', 'tp'), may hold values from -6 to 6
- response_values: bfloat16 [8192, 1024], P('seq', 'tp'), may hold values from -6 to 6
- lengths: int32 [16], replicated, may hold values from 1 to 4096, 8192 in all
- out_weight: bfloat16 [5120, 5120], P('tp'), may hold values from -0.125 to 0.125
Outputs:
- projected: bfloat16 [8192, 5120], P('seq', 'tp')
Inputs may be any that keep to these rules, and one draw needn't show every extreme that they name: `queries`: in a few rows a query head may be a multiple of a prompt key of its key head. 16 lengths that sum to 8192; the longest has exactly 4096 tokens.
All inputs are finite; a program needn't handle non-finite values.
Results may differ from a plain program's by a relative error of at most 0.014.
Values may be sent and summed in bfloat16 or wider, within the bound.
A program may use at most 192 MiB of HBM per device.

v0:
```python
import jax
import jax.numpy as jnp
from jax import lax
from jax.sharding import PartitionSpec as P

HEADS = 40
KVH = 8
HD = 128


def segment_layout(lengths, first_row, row_count):
    positions = first_row + jnp.arange(row_count, dtype=jnp.int32)
    seg_ends = jnp.cumsum(lengths)
    seg_starts = seg_ends - lengths
    inside = (positions[:, None] >= seg_starts[None, :]) & (positions[:, None] < seg_ends[None, :])
    own_start = jnp.sum(jnp.where(inside, seg_starts[None, :], 0), axis=1)
    return (positions, own_start)


def update_state(running, grouped, key_block, value_block, visible, scale_factor):
    maximum, summed, weighted = running
    scores = (
        jnp.einsum("rkgd,nkd->rkgn", grouped, key_block, preferred_element_type=jnp.float32)
        * scale_factor
    )
    if visible is not None:
        scores = jnp.where(visible[:, None, None, :], scores, -jnp.inf)
    new_max = jnp.maximum(maximum, jnp.max(scores, axis=3))
    weights = jnp.exp(scores - new_max[..., None])
    rescale = jnp.exp(maximum - new_max)
    rounded = weights.astype(jnp.bfloat16)
    summed = summed * rescale + jnp.sum(weights, axis=3)
    weighted = weighted * rescale[..., None] + jnp.einsum(
        "rkgn,nkd->rkgd", rounded, value_block, preferred_element_type=jnp.float32
    )
    return (new_max, summed, weighted)


def per_device(
    queries, prompt_keys, prompt_values, response_keys, response_values, lengths, out_weight
):
    row_count = queries.shape[0]
    kv_local = prompt_keys.shape[1] // HD
    group_size = HEADS // KVH
    scale_factor = HD ** (-0.5)
    grouped = queries.reshape(row_count, kv_local, group_size, HD)
    first_row = lax.axis_index("seq") * row_count
    positions, own_start = segment_layout(lengths, first_row, row_count)
    softmax_state = (
        jnp.full((row_count, kv_local, group_size), -jnp.inf, jnp.float32),
        jnp.zeros((row_count, kv_local, group_size), jnp.float32),
        jnp.zeros((row_count, kv_local, group_size, HD), jnp.float32),
    )
    prompt_pair = jnp.stack([prompt_keys, prompt_values])
    fragment = lax.all_gather(prompt_pair, "seq", axis=1, tiled=True)
    frag_rows = fragment.shape[1]
    key_block = fragment[0].reshape(frag_rows, kv_local, HD)
    value_block = fragment[1].reshape(frag_rows, kv_local, HD)
    softmax_state = update_state(softmax_state, grouped, key_block, value_block, None, scale_factor)
    response_pair = jnp.stack([response_keys, response_values])
    fragment = lax.all_gather(response_pair, "seq", axis=1, tiled=True)
    frag_rows = fragment.shape[1]
    key_pos = jnp.arange(frag_rows, dtype=jnp.int32)
    visible = (key_pos[None, :] <= positions[:, None]) & (key_pos[None, :] >= own_start[:, None])
    key_block = fragment[0].reshape(frag_rows, kv_local, HD)
    value_block = fragment[1].reshape(frag_rows, kv_local, HD)
    softmax_state = update_state(
        softmax_state, grouped, key_block, value_block, visible, scale_factor
    )
    maximum, summed, weighted = softmax_state
    attended = (
        (weighted / summed[..., None])
        .astype(jnp.bfloat16)
        .reshape(row_count, kv_local * group_size * HD)
    )
    partial_out = jnp.dot(attended, out_weight, preferred_element_type=jnp.float32)
    return lax.psum_scatter(partial_out.astype(jnp.bfloat16), "tp", scatter_dimension=1, tiled=True)


def solution(mesh):
    in_specs = (
        P("seq", "tp"),
        P("seq", "tp"),
        P("seq", "tp"),
        P("seq", "tp"),
        P("seq", "tp"),
        P(),
        P("tp", None),
    )
    out_specs = P("seq", "tp")
    return jax.shard_map(
        per_device, mesh=mesh, in_specs=in_specs, out_specs=out_specs, check_vma=False
    )
```

profile of v0, /device:TPU:32, one launch (start us, length us, event | category | flops | bytes accessed | tf_op | source)
XLA Modules:
  0.0 299.7 jit_solution(3897833121249140386)
XLA Ops:
  6.5 0.0 all-gather.3.cloned.1.call-start
  6.5 1.4 pad_maximum_fusion.1
  7.9 0.0 all-gather.3.cloned.1.call-update
  8.0 0.0 all-gather.5.cloned.1.call-start
  8.0 1.5 pad_maximum_fusion
  9.6 0.0 all-gather.5.cloned.1.call-update
  9.6 0.0 reduce-scatter.4.cloned.1.call-start
  9.6 0.7 copy.35
  10.4 0.1 reduce.4
  10.5 0.7 sub.50
  11.2 1.1 copy.31
  12.3 0.1 select_reduce_fusion
  12.4 2.0 fusion.13
  14.5 0.0 copy-start.2
  14.5 77.3 %all-gather.3.cloned.1.call-done = bf16[2,4096,128]{2,1,0:T(8,128)(2,1)} async-done(((bf16[2,128,128]{2,1,0:T(8,128)(2,1)}), bf16[2,4096,128]{2,1,0:T(8,128)(2,1)}) %all-gather.3.cloned.1.call-update) | async-done | bytes 2097168 | tf_op jit(solution)/shard_map/all_gather | solution.py:55
  91.8 4.1 %bitcast_reduce_fusion = (f32[256,5]{0,1:T(8,128)S(1)}, f32[4096,256,5]{1,0,2:T(8,128)S(1)}) fusion(bf16[256,5,128]{0,2,1:T(8,128)(2,1)S(1)} %bitcast.121, bf16[2,4096,128]{2,1,0:T(8,128)(2,1)} %all-gather.3.cloned.1.call-done), kind=kOutput, calls=%fused_computation.7 | convolution fusion | flops 1352661760 | bytes 22352896 | tf_op jit(solution)/shard_map/rkgd,nkd->rkgn/dot_general | solution.py:23
  95.9 0.0 copy-start
  95.9 7.0 %copy-done = f32[4096,256,5]{1,0,2:T(8,128)} copy-done((f32[4096,256,5]{1,0,2:T(8,128)}, f32[4096,256,5]{1,0,2:T(8,128)S(1)}, u32[]{:S(2)}) %copy-start) | copy-done | bytes 20971544
  102.9 3.8 %fusion.8 = f32[256,5]{0,1:T(8,128)S(1)} fusion(f32[4096,256,5]{1,0,2:T(8,128)S(1)} %get-tuple-element.9, f32[256,5]{0,1:T(8,128)S(1)} %get-tuple-element.8), kind=kLoop, calls=%fused_computation.11 | loop fusion | flops 15727360 | bytes 20981760 | tf_op jit(solution)/shard_map/reduce_sum | solution.py:32
  106.7 71.5 %all-gather.5.cloned.1.call-done = bf16[2,8192,128]{2,1,0:T(8,128)(2,1)} async-done(((bf16[2,256,128]{2,1,0:T(8,128)(2,1)}), bf16[2,8192,128]{2,1,0:T(8,128)(2,1)}) %all-gather.5.cloned.1.call-update) | async-done | bytes 4194320 | tf_op jit(solution)/shard_map/all_gather | solution.py:61
  178.2 0.0 copy-done.2
  178.2 18.1 %fusion.2 = (f32[256,5]{0,1:T(8,128)S(1)}, f32[8192,256,5]{1,0,2:T(8,128)}) fusion(pred[256,8192]{0,1:T(8,128)(4,1)S(1)} %fusion.13, bf16[256,5,128]{0,2,1:T(8,128)(2,1)S(1)} %bitcast.122, bf16[2,8192,128]{2,1,0:T(8,128)(2,1)} %all-gather.5.cloned.1.call-done), kind=kOutput, calls=%fused_computation.4 | convolution fusion | flops 2715810560 | bytes 46470144 | tf_op jit(solution)/shard_map/rkgd,nkd->rkgn/dot_general | solution.py:23
  196.4 0.0 copy-start.1
  196.4 18.6 %fusion = f32[256,5]{0,1:T(8,128)S(1)} fusion(f32[8192,256,5]{1,0,2:T(8,128)} %get-tuple-element.11, f32[256,5]{0,1:T(8,128)S(1)} %max.17, pred[256,8192]{0,1:T(8,128)(4,1)} %copy-done.2), kind=kLoop, calls=%fused_computation.2 | loop fusion | flops 41941760 | bytes 44050432 | tf_op jit(solution)/shard_map/reduce_sum | solution.py:32
  215.0 1.1 copy-done.1
  216.1 4.5 %fusion.27 = f32[1,128,256,5]{2,1,3,0:T(8,128)S(1)} fusion(f32[4096,256,5]{1,0,2:T(8,128)S(1)} %copy-done.1, f32[256,5]{0,1:T(8,128)S(1)} %get-tuple-element.8, bf16[2,4096,128]{2,1,0:T(8,128)(2,1)} %all-gather.3.cloned.1.call-done, f32[256,5]{0,1:T(8,128)S(1)} %get-tuple-element.6, f32[256,5]{0,1:T(8,128)S(1)} %get-tuple-element.7), kind=kOutput, calls=%fused_computation.26 | convolution fusion | flops 1358233600 | bytes 22690816 | tf_op jit(solution)/shard_map/rkgn,nkd->rkgd/dot_general | solution.py:33
  220.6 18.8 %fusion.34 = bf16[1,128,256,5]{2,1,3,0:T(8,128)(2,1)S(1)} fusion(f32[1,128,256,5]{2,1,3,0:T(8,128)S(1)} %fusion.27, f32[8192,256,5]{1,0,2:T(8,128)} %get-tuple-element.11, f32[256,5]{0,1:T(8,128)S(1)} %max.17, pred[256,8192]{0,1:T(8,128)(4,1)} %copy-done.2, bf16[2,8192,128]{2,1,0:T(8,128)(2,1)} %all-gather.5.cloned.1.call-done, ...), kind=kOutput, calls=%fused_computation.31 | convolution fusion | flops 2726789120 | bytes 47130624 | tf_op jit(solution)/shard_map/rkgn,nkd->rkgd/dot_general | solution.py:33
  239.3 5.1 %convolution_convert_fusion = bf16[256,5120]{1,0:T(8,128)(2,1)S(1)} fusion(bf16[256,640]{0,1:T(8,128)(2,1)S(1)} %bitcast.123, bf16[640,5120]{1,0:T(8,128)(2,1)} %param.13), kind=kOutput, calls=%fused_computation.18 | convolution fusion | flops 1679032320 | bytes 9502720 | tf_op jit(solution)/shard_map/dot_general | solution.py:76
  244.4 2.6 copy.47
  247.0 0.0 reduce-scatter.4.cloned.1.call-update
  247.0 44.3 %reduce-scatter.4.cloned.1.call-done = bf16[640,256]{1,0:T(8,128)(2,1)} async-done(((bf16[5120,256]{1,0:T(8,128)(2,1)}), bf16[640,256]{1,0:T(8,128)(2,1)}) %reduce-scatter.4.cloned.1.call-update) | async-done | bytes 327696
  291.3 1.9 copy.48
  (4 shorter events, 0.1 us)
Async XLA Ops:
  6.5 85.3 %all-gather.3.cloned.1.call-start = ((), (), s32[]{:S(2)}) async-start(), calls=%async_computation.1 | async-start | bytes 2162688 | tf_op jit(solution)/shard_map/all_gather | solution.py:55
  8.0 170.3 %all-gather.5.cloned.1.call-start = ((), (), s32[]{:S(2)}) async-start(), calls=%async_computation.2 | async-start | bytes 4325376 | tf_op jit(solution)/shard_map/all_gather | solution.py:61
  9.6 281.7 %reduce-scatter.4.cloned.1.call-start = ((), (), s32[]{:S(2)}) async-start(), calls=%async_computation.3 | async-start | bytes 2949120
  14.5 163.8 %copy-start.2 = (pred[256,8192]{0,1:T(8,128)(4,1)}, pred[256,8192]{0,1:T(8,128)(4,1)S(1)}, u32[]{:S(2)}) copy-start(pred[256,8192]{0,1:T(8,128)(4,1)S(1)} %fusion.13) | copy-start | bytes 6291460
  95.9 7.0 %copy-start = (f32[4096,256,5]{1,0,2:T(8,128)}, f32[4096,256,5]{1,0,2:T(8,128)S(1)}, u32[]{:S(2)}) copy-start(f32[4096,256,5]{1,0,2:T(8,128)S(1)} %get-tuple-element.9) | copy-start | bytes 62914564
  196.4 19.7 %copy-start.1 = (f32[4096,256,5]{1,0,2:T(8,128)S(1)}, f32[4096,256,5]{1,0,2:T(8,128)}, u32[]{:S(2)}) copy-start(f32[4096,256,5]{1,0,2:T(8,128)} %copy-done) | copy-start | bytes 62914564
Sparse Core Ops, SparseCore 0:
  10.2 81.6 all-gather.2
  94.6 83.5 all-gather.4
  247.2 44.0 reduce-scatter.3
where the time goes:
time: 300 us
  waiting for transfers between devices  193 us (64%)
  matrix products  50.5 us (17%)
  other arithmetic  28.3 us (9%)
  local copies, waits for them, and re-layouts  14.4 us (5%)
  between operations  13.2 us (4%)
    all_gather x1, waiting for transfers between devices, per_device(): fragment = lax.all_gather(prompt_pair, 'seq', axis=1, tiled=True)  77.3 us
    all_gather x1, waiting for transfers between devices, per_device(): fragment = lax.all_gather(response_pair, 'seq', axis=1, tiled=True)  71.5 us
    unnamed x4, waiting for transfers between devices  44.3 us
    dot_general x2, matrix products, update_state(): jnp.einsum('rkgn,nkd->rkgd', rounded, value_block, preferred_element_type...  23.2 us
    reduce_sum x2, other arithmetic, update_state(): summed = summed * rescale + jnp.sum(weights, axis=3)  22.5 us
    dot_general x2, matrix products, update_state(): jnp.einsum('rkgd,nkd->rkgn', grouped, key_block, preferred_element_type=j...  22.2 us
    unnamed x9, local copies, waits for them, and re-layouts  13.6 us
  transfers between devices with their start and end apart: 3, of which 3 were waited for; matrix products, arithmetic and copies ran while one was open for 5% of the time, Pallas kernels for 0%

commit v1 on v0

--- a/solution.py
+++ b/solution.py
@@ -58,7 +58,9 @@
     value_block = fragment[1].reshape(frag_rows, kv_local, HD)
     softmax_state = update_state(softmax_state, grouped, key_block, value_block, None, scale_factor)
     response_pair = jnp.stack([response_keys, response_values])
-    fragment = lax.all_gather(response_pair, "seq", axis=1, tiled=True)
+    fragment = jnp.concatenate(
+        lax.all_to_all(jnp.stack([response_pair] * lax.axis_size("seq")), "seq", 0, 0), axis=1
+    )
     frag_rows = fragment.shape[1]
     key_pos = jnp.arange(frag_rows, dtype=jnp.int32)
     visible = (key_pos[None, :] <= positions[:, None]) & (key_pos[None, :] >= own_start[:, None])

time: 300 us -> 274 us (0.913)
  waiting for transfers between devices: 193 us -> 148 us
  starting transfers between devices: 0.09 us -> 11.5 us
  matrix products: 50.5 us -> 55.8 us
  local copies, waits for them, and re-layouts: 14.4 us -> 19.4 us
    all_gather x1 -> x0, waiting for transfers between devices: 71.5 us -> none  [per_device(): fragment = lax.all_gather(response_pair, 'seq', axis=1, tiled=True)]
    all_gather x1, waiting for transfers between devices: 77.3 us -> 101 us  [per_device(): fragment = lax.all_gather(prompt_pair, 'seq', axis=1, tiled=True)]
    all_to_all x0 -> x1, starting transfers between devices: none -> 11.4 us  [per_device(): lax.all_to_all(jnp.stack([response_pair] * lax.axis_size('seq')), 'seq',...]
    dot_general x2, matrix products: 23.2 us -> 28.5 us  [update_state(): jnp.einsum('rkgn,nkd->rkgd', rounded, value_block, preferred_element_type...]
    slice x0 -> x1, local copies, waits for them, and re-layouts: none -> 4.72 us  [per_device(): value_block = fragment[1].reshape(frag_rows, kv_local, HD)]
    unnamed x4 -> x3, waiting for transfers between devices: 44.3 us -> 47 us
    unnamed x9 -> x15, local copies, waits for them, and re-layouts: 13.6 us -> 11.6 us
  transfers between devices with their start and end apart: 3 -> 3, of which waited for: 3 -> 2; matrix products, arithmetic and copies ran while one was open for 5% -> 4% of each run, Pallas kernels for 0% -> 0%
where the time goes in v1:
time: 274 us
  waiting for transfers between devices  148 us (54%)
  matrix products  55.8 us (20%)
  other arithmetic  25.6 us (9%)
  local copies, waits for them, and re-layouts  19.4 us (7%)
  between operations  13.5 us (5%)
  starting transfers between devices  11.5 us (4%)
    all_gather x1, waiting for transfers between devices, per_device(): fragment = lax.all_gather(prompt_pair, 'seq', axis=1, tiled=True)  101 us
    unnamed x3, waiting for transfers between devices  47 us
    dot_general x2, matrix products, update_state(): jnp.einsum('rkgn,nkd->rkgd', rounded, value_block, preferred_element_type...  28.5 us
    dot_general x2, matrix products, update_state(): jnp.einsum('rkgd,nkd->rkgn', grouped, key_block, preferred_element_type=j...  22.2 us
    reduce_sum x2, other arithmetic, update_state(): summed = summed * rescale + jnp.sum(weights, axis=3)  21.8 us
    unnamed x15, local copies, waits for them, and re-layouts  11.6 us
    all_to_all x1, starting transfers between devices, per_device(): lax.all_to_all(jnp.stack([response_pair] * lax.axis_size('seq')), 'seq',...  11.4 us
  transfers between devices with their start and end apart: 3, of which 2 were waited for; matrix products, arithmetic and copies ran while one was open for 4% of the time, Pallas kernels for 0%

profile of v1, /device:TPU:32, one launch (start us, length us, event | category | flops | bytes accessed | tf_op | source)
XLA Modules:
  0.0 273.6 jit_solution(4689285555307944694)
XLA Ops:
  6.5 0.0 copy-start.4
  6.5 0.0 copy-start.3
  6.5 0.0 copy-start.5
  6.5 0.0 copy-start.2
  6.5 0.9 pad_maximum_fusion
  7.5 3.0 %stack.20 = bf16[32,2,256,128]{3,2,1,0:T(8,128)(2,1)} broadcast(bf16[2,256,128]{2,1,0:T(8,128)(2,1)S(1)} %pad_maximum_fusion), dimensions={1,2,3} | broadcast | bytes 4325376 | tf_op jit(solution)/shard_map/stack | solution.py:62
  10.5 11.4 %all-to-all-start = ((bf16[32,2,256,128]{3,2,1,0:T(8,128)(2,1)}), bf16[32,2,256,128]{3,2,1,0:T(8,128)(2,1)}, u32[]{:S(2)}, u32[]{:S(2)}) async-start(bf16[32,2,256,128]{3,2,1,0:T(8,128)(2,1)} %stack.20), calls=%async_computation | async-start | bytes 8388608 | tf_op jit(solution)/shard_map/all_to_all | solution.py:62
  21.9 0.0 all-gather.2.cloned.1.call-start
  21.9 0.0 copy-done.4
  21.9 0.0 copy-done.3
  22.0 0.6 pad_maximum_fusion.1
  22.6 0.0 all-gather.2.cloned.1.call-update
  22.6 0.0 reduce-scatter.4.cloned.1.call-start
  22.7 0.0 copy-done.5
  22.7 0.1 copy.35
  22.8 0.1 reduce.4
  22.9 0.0 copy-done.2
  22.9 0.2 copy.31
  23.1 0.1 select_reduce_fusion
  23.2 2.0 fusion.13
  25.3 100.7 %all-gather.2.cloned.1.call-done = bf16[2,4096,128]{2,1,0:T(8,128)(2,1)} async-done(((bf16[2,128,128]{2,1,0:T(8,128)(2,1)}), bf16[2,4096,128]{2,1,0:T(8,128)(2,1)}) %all-gather.2.cloned.1.call-update) | async-done | bytes 2097168 | tf_op jit(solution)/shard_map/all_gather | solution.py:55
  126.0 4.1 %bitcast_reduce_fusion = (f32[256,5]{0,1:T(8,128)S(1)}, f32[4096,256,5]{1,0,2:T(8,128)S(1)}) fusion(bf16[256,5,128]{0,2,1:T(8,128)(2,1)S(1)} %bitcast.114, bf16[2,4096,128]{2,1,0:T(8,128)(2,1)} %all-gather.2.cloned.1.call-done), kind=kOutput, calls=%fused_computation.7 | convolution fusion | flops 1352661760 | bytes 22352896 | tf_op jit(solution)/shard_map/rkgd,nkd->rkgn/dot_general | solution.py:23
  130.1 0.0 copy-start
  130.1 7.0 %copy-done = f32[4096,256,5]{1,0,2:T(8,128)} copy-done((f32[4096,256,5]{1,0,2:T(8,128)}, f32[4096,256,5]{1,0,2:T(8,128)S(1)}, u32[]{:S(2)}) %copy-start) | copy-done | bytes 20971544
  137.1 3.8 %fusion.8 = f32[256,5]{0,1:T(8,128)S(1)} fusion(f32[4096,256,5]{1,0,2:T(8,128)S(1)} %get-tuple-element.11, f32[256,5]{0,1:T(8,128)S(1)} %get-tuple-element.10), kind=kLoop, calls=%fused_computation.11 | loop fusion | flops 15727360 | bytes 20981760 | tf_op jit(solution)/shard_map/reduce_sum | solution.py:32
  140.9 0.0 all-to-all-done
  140.9 4.7 %fusion.39 = (bf16[1,32,256,128]{3,2,0,1:T(8,128)(2,1)}, bf16[1,32,256,128]{3,2,0,1:T(8,128)(2,1)}) fusion(bf16[2,32,256,128]{3,2,0,1:T(8,128)(2,1)} %bitcast.15), kind=kLoop, calls=%fused_computation.39 | loop fusion | bytes 8388608 | tf_op jit(solution)/shard_map/slice | solution.py:68
  145.6 18.1 %fusion.2 = (f32[256,5]{0,1:T(8,128)S(1)}, f32[8192,256,5]{1,0,2:T(8,128)}) fusion(pred[256,8192]{0,1:T(8,128)(4,1)S(1)} %fusion.13, bf16[8192,128,1]{1,0,2:T(8,128)(2,1)} %bitcast.113, bf16[256,5,128]{0,2,1:T(8,128)(2,1)S(1)} %bitcast.115), kind=kOutput, calls=%fused_computation.4 | convolution fusion | flops 2715810560 | bytes 46470144 | tf_op jit(solution)/shard_map/rkgd,nkd->rkgn/dot_general | solution.py:23
  163.7 0.0 copy-start.1
  163.7 17.9 %fusion = f32[256,5]{0,1:T(8,128)S(1)} fusion(f32[8192,256,5]{1,0,2:T(8,128)} %get-tuple-element.13, f32[256,5]{0,1:T(8,128)S(1)} %max.17, pred[256,8192]{0,1:T(8,128)(4,1)S(1)} %fusion.13), kind=kLoop, calls=%fused_computation.2 | loop fusion | flops 41941760 | bytes 44050432 | tf_op jit(solution)/shard_map/reduce_sum | solution.py:32
  181.7 0.0 copy-done.1
  181.7 9.2 %fusion.26 = f32[1,128,256,5]{2,1,3,0:T(8,128)S(1)} fusion(f32[4096,256,5]{1,0,2:T(8,128)} %copy-done, f32[256,5]{0,1:T(8,128)S(1)} %get-tuple-element.10, bf16[2,4096,128]{2,1,0:T(8,128)(2,1)S(1)} %copy-done.1, f32[256,5]{0,1:T(8,128)S(1)} %get-tuple-element.6, f32[256,5]{0,1:T(8,128)S(1)} %get-tuple-element.9), kind=kOutput, calls=%fused_computation.23 | convolution fusion | flops 1358233600 | bytes 22700032 | tf_op jit(solution)/shard_map/rkgn,nkd->rkgd/dot_general | solution.py:33
  191.0 19.3 %fusion.33 = bf16[1,128,256,5]{2,1,3,0:T(8,128)(2,1)S(1)} fusion(f32[1,128,256,5]{2,1,3,0:T(8,128)S(1)} %fusion.26, bf16[8192,128,1]{1,0,2:T(8,128)(2,1)} %bitcast.112, f32[8192,256,5]{1,0,2:T(8,128)} %get-tuple-element.13, f32[256,5]{0,1:T(8,128)S(1)} %max.17, pred[256,8192]{0,1:T(8,128)(4,1)S(1)} %fusion.13, f32[256,5]{0,1:T(8,128)S(1)} %get-tuple-element.5), kind=kOutput, calls=%fused_computation.28 | convolution fusion | flops 2726789120 | bytes 47130624 | tf_op jit(solution)/shard_map/rkgn,nkd->rkgd/dot_general | solution.py:33
  210.2 5.1 %convolution_convert_fusion = bf16[256,5120]{1,0:T(8,128)(2,1)S(1)} fusion(bf16[256,640]{0,1:T(8,128)(2,1)S(1)} %bitcast.116, bf16[640,5120]{1,0:T(8,128)(2,1)} %param.13), kind=kOutput, calls=%fused_computation.18 | convolution fusion | flops 1679032320 | bytes 9502720 | tf_op jit(solution)/shard_map/dot_general | solution.py:78
  215.4 2.6 copy.46
  217.9 0.0 reduce-scatter.4.cloned.1.call-update
  218.0 46.9 %reduce-scatter.4.cloned.1.call-done = bf16[640,256]{1,0:T(8,128)(2,1)} async-done(((bf16[5120,256]{1,0:T(8,128)(2,1)}), bf16[640,256]{1,0:T(8,128)(2,1)}) %reduce-scatter.4.cloned.1.call-update) | async-done | bytes 327696
  264.9 1.9 copy.47
  (5 shorter events, 0.1 us)
Async XLA Ops:
  6.5 15.4 %copy-start.4 = (bf16[128,128]{1,0:T(8,128)(2,1)S(1)}, bf16[128,128]{1,0:T(8,128)(2,1)}, u32[]{:S(2)}) copy-start(bf16[128,128]{1,0:T(8,128)(2,1)} %param.8) | copy-start | bytes 98308
  6.5 15.4 %copy-start.3 = (bf16[128,128]{1,0:T(8,128)(2,1)S(1)}, bf16[128,128]{1,0:T(8,128)(2,1)}, u32[]{:S(2)}) copy-start(bf16[128,128]{1,0:T(8,128)(2,1)} %param.9) | copy-start | bytes 98308
  6.5 16.1 %copy-start.5 = (s32[16]{0:T(128)S(1)}, s32[16]{0:T(128)}, u32[]{:S(2)}) copy-start(s32[16]{0:T(128)} %param.12) | copy-start | bytes 196
  6.5 16.4 %copy-start.2 = (bf16[256,640]{1,0:T(8,128)(2,1)S(1)}, bf16[256,640]{1,0:T(8,128)(2,1)}, u32[]{:S(2)}) copy-start(bf16[256,640]{1,0:T(8,128)(2,1)} %param.7) | copy-start | bytes 983044
  10.5 130.4 %all-to-all-start = ((bf16[32,2,256,128]{3,2,1,0:T(8,128)(2,1)}), bf16[32,2,256,128]{3,2,1,0:T(8,128)(2,1)}, u32[]{:S(2)}, u32[]{:S(2)}) async-start(bf16[32,2,256,128]{3,2,1,0:T(8,128)(2,1)} %stack.20), calls=%async_computation | async-start | bytes 8388608 | tf_op jit(solution)/shard_map/all_to_all | solution.py:62
  21.9 104.1 %all-gather.2.cloned.1.call-start = ((), (), s32[]{:S(2)}) async-start(), calls=%async_computation.2 | async-start | bytes 2162688 | tf_op jit(solution)/shard_map/all_gather | solution.py:55
  22.6 242.3 %reduce-scatter.4.cloned.1.call-start = ((), (), s32[]{:S(2)}) async-start(), calls=%async_computation.3 | async-start | bytes 2949120
  130.1 7.0 %copy-start = (f32[4096,256,5]{1,0,2:T(8,128)}, f32[4096,256,5]{1,0,2:T(8,128)S(1)}, u32[]{:S(2)}) copy-start(f32[4096,256,5]{1,0,2:T(8,128)S(1)} %get-tuple-element.11) | copy-start | bytes 62914564
  163.7 18.0 %copy-start.1 = (bf16[2,4096,128]{2,1,0:T(8,128)(2,1)S(1)}, bf16[2,4096,128]{2,1,0:T(8,128)(2,1)}, u32[]{:S(2)}) copy-start(bf16[2,4096,128]{2,1,0:T(8,128)(2,1)} %all-gather.2.cloned.1.call-done) | copy-start | bytes 6291460
Sparse Core Ops, SparseCore 0:
  25.5 100.4 all-gather.1
  218.1 46.7 reduce-scatter.3
